TPU v7x, 32 devices: a whole 2x2x4 slice. The times are simulated.
32 devices in a mesh: dom: 2 (over y), row: 4 (over z), sub: 2 (over x), rep: 2 (over core).
Axes of the slice: x: 2, y: 2, z: 4, core: 2. Of those that a mesh axis runs over, the one named last changes fastest.
Arguments:
- vectors: bfloat16 [28672, 768], P(('dom', 'row', 'sub', 'rep')), parts along dimension 0, may hold values from -150 to 150
- rotation: bfloat16 [1536, 768], P('dom'), parts along dimension 0, may hold values from -0.21875 to 0.21875
- codebooks: float32 [96, 256, 16], P(('dom', 'sub')), parts along dimension 0, may hold values from -8 to 8
Outputs:
- reconstruction: bfloat16 [28672, 768], P(('dom', 'row', 'sub', 'rep')), parts along dimension 0
- new_codebooks: float32 [96, 256, 16], P(('dom', 'sub')), parts along dimension 0
- cross_cov: float32 [1536, 768], P(('dom', 'sub')), parts along dimension 0
There are 2 independent parts, one for each index of `dom`. A program takes and returns all parts, laid end to end along the dimension named above; each array names one. Nothing has to cross between parts.
All inputs are finite; a program needn't handle non-finite values.
Results may differ from a plain program's by a relative error of at most 0.012.
Values may be sent and summed in bfloat16 or wider, within the bound.
No kernel may reach another device: no remote copies, remote signals or barrier semaphores. Data moves between devices by JAX's collectives and lax.ppermute only.
A program may use at most 64 MiB of HBM per device.

v0:
```python
import jax
import jax.numpy as jnp
from jax import lax
from jax.sharding import PartitionSpec as P

SUBDIM = 16
softness_scale = 4.0


def quantize_rows(block, codebook):
    block = block.astype(jnp.float32)
    cross_product = jnp.dot(codebook, block, precision=lax.Precision.HIGHEST)
    squared_norms = jnp.sum(codebook * codebook, axis=1)
    affinity_scores = (2.0 * cross_product - squared_norms[:, None]) / softness_scale
    weights = jax.nn.softmax(affinity_scores, axis=0)
    recon = jnp.dot(codebook.T, weights, precision=lax.Precision.HIGHEST)
    sums = lax.dot_general(
        weights, block, (((1,), (1,)), ((), ())), precision=lax.Precision.HIGHEST
    )
    counts = jnp.sum(weights, axis=1)
    return (recon, sums, counts)


def on_device(vectors, rotation, codebooks):
    row_count = vectors.shape[0]
    width = vectors.shape[1]
    groups = lax.axis_size("sub")
    group_width = width // groups
    rotated_t = lax.dot_general(
        rotation, vectors, (((0,), (1,)), ((), ())), preferred_element_type=jnp.float32
    ).astype(jnp.bfloat16)
    grouped = rotated_t.reshape(groups, group_width, row_count)
    received = lax.all_to_all(grouped, "sub", split_axis=0, concat_axis=2, tiled=True)
    columns = received.shape[2]
    blocks = received.reshape(group_width // SUBDIM, SUBDIM, columns)
    recon, sums_local, counts_local = lax.map(
        lambda pair: quantize_rows(pair[0], pair[1]), (blocks, codebooks)
    )
    recon_sent = recon.astype(jnp.bfloat16).reshape(1, group_width, columns)
    returned = lax.all_to_all(recon_sent, "sub", split_axis=2, concat_axis=0, tiled=True)
    recon_t = returned.reshape(width, row_count)
    total = row_count * lax.axis_size("row") * groups * lax.axis_size("rep")
    code_sums, counts = lax.psum((sums_local, counts_local), ("row", "rep"))
    partial_term = lax.dot_general(
        vectors, recon_t, (((0,), (1,)), ((), ())), preferred_element_type=jnp.float32
    )
    whole_cross = lax.psum(partial_term, ("row", "sub", "rep"))
    cross_rows = lax.dynamic_slice_in_dim(
        whole_cross, lax.axis_index("sub") * group_width, group_width, 0
    )
    new_codebooks = (code_sums + codebooks) / (counts[:, :, None] + 1.0)
    reconstruction = recon_t.T
    return (reconstruction, new_codebooks, cross_rows / total)


def solution(mesh):
    placed = (P(("dom", "row", "sub", "rep"), None), P("dom", None), P(("dom", "sub"), None, None))
    return jax.shard_map(
        on_device,
        mesh=mesh,
        in_specs=placed,
        out_specs=(
            P(("dom", "row", "sub", "rep"), None),
            P(("dom", "sub"), None, None),
            P(("dom", "sub"), None),
        ),
        check_vma=False,
    )
```

profile of v0, /device:TPU:0, one launch (start us, length us, event | category | flops | bytes accessed | tf_op | source)
XLA Modules:
  0.0 368.6 jit_solution(16869227199885064852)
XLA Ops:
  8.5 3.8 %convolution_convert_fusion = bf16[768,896]{1,0:T(8,128)(2,1)} fusion(bf16[768,768]{1,0:T(8,128)(2,1)} %param.6, bf16[896,768]{1,0:T(8,128)(2,1)S(1)} %copy-done), kind=kOutput, calls=%fused_computation.25 | convolution fusion | flops 1057652736 | bytes 3932160 | tf_op jit(solution)/shard_map/dot_general | solution.py:29
  12.3 4.2 %all-to-all-start = ((bf16[2,384,896]{2,1,0:T(8,128)(2,1)}), bf16[2,384,896]{2,1,0:T(8,128)(2,1)S(1)}, u32[]{:S(2)}, u32[]{:S(2)}) async-start(bf16[2,384,896]{2,1,0:T(8,128)(2,1)} %bitcast.68), calls=%async_computation | async-start | bytes 2752512 | tf_op jit(solution)/shard_map/all_to_all | solution.py:33
  16.5 18.0 %all-to-all-done = bf16[2,384,896]{2,1,0:T(8,128)(2,1)S(1)} async-done(((bf16[2,384,896]{2,1,0:T(8,128)(2,1)}), bf16[2,384,896]{2,1,0:T(8,128)(2,1)S(1)}, u32[]{:S(2)}, u32[]{:S(2)}) %all-to-all-start) | async-done | bytes 1376288 | tf_op jit(solution)/shard_map/all_to_all | solution.py:33
  34.5 2.5 copy.16
  37.0 3.5 reshape.26
  40.5 130.4 %while.14 = (s32[]{:T(128)}, bf16[24,16,1792]{2,1,0:T(8,128)(2,1)}, f32[24,256,16]{1,2,0:T(8,128)}, f32[24,256]{1,0:T(8,128)S(1)}, f32[24,256,16]{1,2,0:T(8,128)...) while((s32[]{:T(128)}, bf16[24,16,1792]{2,1,0:T(8,128)(2,1)}, f32[24,256,16]{1,2,0:T(8,128)}, ...), condition=%wide.region_5.6_spmd, body=%wide.region_0.5_spmd.sunk | while | flops 270209024 | bytes 9546853 | solution.py:36
  41.9 1.8 fusion.43
  47.4 1.8 fusion.43
  49.2 1.8 fusion.44
  52.8 1.8 fusion.43
  58.2 1.8 fusion.43
  63.7 1.8 fusion.43
  69.1 1.8 fusion.43
  70.9 1.8 fusion.44
  74.5 1.8 fusion.43
  80.0 1.8 fusion.43
  81.8 1.8 fusion.44
  85.4 1.8 fusion.43
  90.8 1.8 fusion.43
  96.3 1.8 fusion.43
  101.7 1.8 fusion.43
  103.5 1.8 fusion.44
  107.1 1.8 fusion.43
  112.6 1.8 fusion.43
  118.0 1.8 fusion.43
  123.4 1.8 fusion.43
  125.2 1.8 fusion.44
  128.9 1.8 fusion.43
  134.3 1.8 fusion.43
  136.1 1.8 fusion.44
  139.7 1.8 fusion.43
  145.2 1.8 fusion.43
  147.0 1.8 fusion.44
  150.6 1.8 fusion.43
  156.0 1.8 fusion.43
  161.5 1.8 fusion.43
  166.9 1.8 fusion.43
  170.9 7.0 %copy.17 = bf16[1,384,1792]{1,0,2:T(2,128)(2,1)} copy(bf16[1,384,1792]{2,1,0:T(8,128)(2,1)} %bitcast.67) | data formatting | bytes 2752512 | tf_op jit(solution)/shard_map/reshape | solution.py:39
  178.4 12.4 %reduce = bf16[1792,384]{1,0:T(8,128)(2,1)S(1)} reduce(bf16[1792,1,384]{2,1,0:T(2,128)(2,1)} %bitcast.61, bf16[]{:T(256)} %broadcast.16), dimensions={1}, to_apply=%bitcast.35.reduce_sub_computation | reduce | bytes 2752514
  192.0 3.6 all-to-all-start.1
  196.7 15.8 %all-to-all-done.1 = bf16[2,2,172032]{2,1,0:T(2,128)(2,1)S(1)} async-done(((bf16[2,2,172032]{2,1,0:T(2,128)(2,1)}), bf16[2,2,172032]{2,1,0:T(2,128)(2,1)S(1)}, u32[]{:S(2)}, u32[]{:S(2)}) %all-to-all-start.1) | async-done | bytes 1376288 | tf_op jit(solution)/shard_map/all_to_all | solution.py:40
  212.5 2.3 reshape.30
  214.8 3.1 copy.21
  219.7 2.8 convolution_bitcast_fusion.2
  222.5 27.0 %psum.22 = f32[24,256]{1,0:T(8,128)S(1)} all-reduce(f32[24,256]{1,0:T(8,128)S(1)} %get-tuple-element.39), channel_id=1, replica_groups=mesh['dom'=2,'row'=4,'sub'=2,'rep'=2] {'row','rep'}, use_global_device_ids=true, to_apply=%region_7.8 | all-reduce | flops 6144 | bytes 49152 | tf_op jit(solution)/shard_map/psum | solution.py:43
  249.5 7.6 %all-reduce.3.cloned.1.call-done = f32[24,256,16]{1,2,0:T(8,128)} async-done(((f32[24,256,16]{1,2,0:T(8,128)}), f32[24,256,16]{1,2,0:T(8,128)}) %all-reduce.3.cloned.1.call-update) | async-done | bytes 393232 | tf_op jit(solution)/shard_map/psum | solution.py:43
  257.1 1.8 add_divide_fusion
  260.4 98.6 %all-reduce.5.cloned.1.call-done = f32[768,768]{0,1:T(8,128)} async-done(((f32[768,768]{0,1:T(8,128)}), f32[768,768]{0,1:T(8,128)}) %all-reduce.5.cloned.1.call-update) | async-done | bytes 2359312 | tf_op jit(solution)/shard_map/psum | solution.py:47
  (155 shorter events, 83.7 us)
Async XLA Ops:
  7.2 1.3 copy-start
  12.3 22.2 %all-to-all-start = ((bf16[2,384,896]{2,1,0:T(8,128)(2,1)}), bf16[2,384,896]{2,1,0:T(8,128)(2,1)S(1)}, u32[]{:S(2)}, u32[]{:S(2)}) async-start(bf16[2,384,896]{2,1,0:T(8,128)(2,1)} %bitcast.68), calls=%async_computation | async-start | bytes 2752512 | tf_op jit(solution)/shard_map/all_to_all | solution.py:33
  37.0 3.5 copy-start.1
  192.0 20.5 %all-to-all-start.1 = ((bf16[2,2,172032]{2,1,0:T(2,128)(2,1)}), bf16[2,2,172032]{2,1,0:T(2,128)(2,1)S(1)}, u32[]{:S(2)}, u32[]{:S(2)}) async-start(bf16[2,2,172032]{2,1,0:T(2,128)(2,1)} %reshape.29), calls=%async_computation.1 | async-start | bytes 2752512 | tf_op jit(solution)/shard_map/all_to_all | solution.py:40
  195.7 61.4 %all-reduce.3.cloned.1.call-start = ((), (), s32[]{:S(2)}) async-start(), calls=%async_computation.2 | async-start | bytes 786432 | tf_op jit(solution)/shard_map/psum | solution.py:43
  196.4 162.6 %all-reduce.5.cloned.1.call-start = ((), (), s32[]{:S(2)}) async-start(), calls=%async_computation.3 | async-start | bytes 4718592 | tf_op jit(solution)/shard_map/psum | solution.py:47
Sparse Core Ops, SparseCore 0:
  199.4 57.6 all-reduce.2
  261.1 97.9 all-reduce.4
where the time goes:
time: 369 us
  waiting for transfers between devices  141 us (38%)
  matrix products  119 us (32%)
  other arithmetic  31.9 us (9%)
  local copies, waits for them, and re-layouts  27.1 us (7%)
  blocking collectives  27 us (7%)
  between operations  14.1 us (4%)
  starting transfers between devices  8.1 us (2%)
    psum x1, waiting for transfers between devices, on_device(): whole_cross = lax.psum(partial_term, ('row', 'sub', 'rep'))  98.6 us
    dot_general x24, matrix products, quantize_rows(): recon = jnp.dot(codebook.T, weights, precision=lax.Precision.HIGHEST)  43.4 us
    dot_general x24, matrix products, quantize_rows(): lax.dot_general(weights, block, (((1,), (1,)), ((), ())), precision=lax.P...  43.1 us
    psum x1, blocking collectives, on_device(): code_sums, counts = lax.psum((sums_local, counts_local), ('row', 'rep'))  27 us
    dot_general x24, matrix products, quantize_rows(): cross_product = jnp.dot(codebook, block, precision=lax.Precision.HIGHEST)  25.8 us
    all_to_all x1, waiting for transfers between devices, on_device(): lax.all_to_all(grouped, 'sub', split_axis=0, concat_axis=2, tiled=True)  18 us
    all_to_all x1, waiting for transfers between devices, on_device(): lax.all_to_all(recon_sent, 'sub', split_axis=2, concat_axis=0, tiled=True)  15.8 us
    unnamed x1, other arithmetic  12.4 us
  transfers between devices with their start and end apart: 4, of which 4 were waited for; matrix products, arithmetic and copies ran while one was open for 4% of the time, Pallas kernels for 0%

commit v1 on v0

--- a/solution.py
+++ b/solution.py
@@ -37,7 +37,10 @@
         lambda pair: quantize_rows(pair[0], pair[1]), (blocks, codebooks)
     )
     recon_sent = recon.astype(jnp.bfloat16).reshape(1, group_width, columns)
-    returned = lax.all_to_all(recon_sent, "sub", split_axis=2, concat_axis=0, tiled=True)
+    returned = jnp.concatenate(
+        lax.all_to_all(jnp.stack(jnp.split(recon_sent, lax.axis_size("sub"), axis=2)), "sub", 0, 0),
+        axis=0,
+    )
     recon_t = returned.reshape(width, row_count)
     total = row_count * lax.axis_size("row") * groups * lax.axis_size("rep")
     code_sums, counts = lax.psum((sums_local, counts_local), ("row", "rep"))

time: 369 us -> 351 us (0.951)
  local copies, waits for them, and re-layouts: 27.1 us -> 12.6 us
  other arithmetic: 31.9 us -> 20.8 us
  waiting for transfers between devices: 141 us -> 148 us
    unnamed x1 -> x0, other arithmetic: 12.4 us -> none
    unnamed x10 -> x5, local copies, waits for them, and re-layouts: 11.4 us -> 2.73 us
    psum x1, waiting for transfers between devices: 7.6 us -> 14.8 us  [on_device(): code_sums, counts = lax.psum((sums_local, counts_local), ('row', 'rep'))]
    reshape x1 -> x0, local copies, waits for them, and re-layouts: 6.95 us -> none  [on_device(): recon_sent = recon.astype(jnp.bfloat16).reshape(1, group_width, columns)]
  transfers between devices with their start and end apart: 4 -> 4, of which waited for: 4 -> 4; matrix products, arithmetic and copies ran while one was open for 4% -> 2% of each run, Pallas kernels for 0% -> 0%
where the time goes in v1:
time: 351 us; the launch traced here: 350 us
  waiting for transfers between devices  148 us (42%)
  matrix products  119 us (34%)
  blocking collectives  27 us (8%)
  other arithmetic  20.8 us (6%)
  between operations  14.1 us (4%)
  local copies, waits for them, and re-layouts  12.6 us (4%)
  starting transfers between devices  7.92 us (2%)
    psum x1, waiting for transfers between devices, on_device(): whole_cross = lax.psum(partial_term, ('row', 'sub', 'rep'))  98.6 us
    dot_general x24, matrix products, quantize_rows(): recon = jnp.dot(codebook.T, weights, precision=lax.Precision.HIGHEST)  43.4 us
    dot_general x24, matrix products, quantize_rows(): lax.dot_general(weights, block, (((1,), (1,)), ((), ())), precision=lax.P...  43.1 us
    psum x1, blocking collectives, on_device(): code_sums, counts = lax.psum((sums_local, counts_local), ('row', 'rep'))  27 us
    dot_general x24, matrix products, quantize_rows(): cross_product = jnp.dot(codebook, block, precision=lax.Precision.HIGHEST)  25.8 us
    all_to_all x1, waiting for transfers between devices, on_device(): lax.all_to_all(grouped, 'sub', split_axis=0, concat_axis=2, tiled=True)  18 us
    all_to_all x1, waiting for transfers between devices, on_device(): lax.all_to_all(jnp.stack(jnp.split(recon_sent, lax.axis_size('sub'), axis...  16 us
    psum x1, waiting for transfers between devices, on_device(): code_sums, counts = lax.psum((sums_local, counts_local), ('row', 'rep'))  14.8 us
  transfers between devices with their start and end apart: 4, of which 4 were waited for; matrix products, arithmetic and copies ran while one was open for 2% of the time, Pallas kernels for 0%

profile of v1, /device:TPU:0, one launch (start us, length us, event | category | flops | bytes accessed | tf_op | source)
XLA Modules:
  0.0 350.2 jit_solution(15157292639542862401)
XLA Ops:
  8.5 3.8 %convolution_convert_fusion = bf16[768,896]{1,0:T(8,128)(2,1)} fusion(bf16[768,768]{1,0:T(8,128)(2,1)} %param.6, bf16[896,768]{1,0:T(8,128)(2,1)S(1)} %copy-done), kind=kOutput, calls=%fused_computation.25 | convolution fusion | flops 1057652736 | bytes 3932160 | tf_op jit(solution)/shard_map/dot_general | solution.py:29
  12.3 4.2 %all-to-all-start = ((bf16[2,384,896]{2,1,0:T(8,128)(2,1)}), bf16[2,384,896]{2,1,0:T(8,128)(2,1)S(1)}, u32[]{:S(2)}, u32[]{:S(2)}) async-start(bf16[2,384,896]{2,1,0:T(8,128)(2,1)} %bitcast.64), calls=%async_computation | async-start | bytes 2752512 | tf_op jit(solution)/shard_map/all_to_all | solution.py:33
  16.5 18.0 %all-to-all-done = bf16[2,384,896]{2,1,0:T(8,128)(2,1)S(1)} async-done(((bf16[2,384,896]{2,1,0:T(8,128)(2,1)}), bf16[2,384,896]{2,1,0:T(8,128)(2,1)S(1)}, u32[]{:S(2)}, u32[]{:S(2)}) %all-to-all-start) | async-done | bytes 1376288 | tf_op jit(solution)/shard_map/all_to_all | solution.py:33
  34.5 2.5 copy.10
  37.0 3.5 %reshape.22 = bf16[24,16,1792]{2,1,0:T(8,128)(2,1)S(1)} reshape(bf16[1,384,2,896]{3,2,1,0:T(2,128)(2,1)} %copy.10) | data formatting | bytes 2752512 | tf_op jit(solution)/shard_map/reshape | solution.py:35
  40.5 130.4 %while.14 = (s32[]{:T(128)}, bf16[24,16,1792]{2,1,0:T(8,128)(2,1)}, f32[24,256,16]{1,2,0:T(8,128)}, f32[24,256]{1,0:T(8,128)S(1)}, f32[24,256,16]{1,2,0:T(8,128)...) while((s32[]{:T(128)}, bf16[24,16,1792]{2,1,0:T(8,128)(2,1)}, f32[24,256,16]{1,2,0:T(8,128)}, ...), condition=%wide.region_5.6_spmd, body=%wide.region_0.5_spmd.sunk | while | flops 270209024 | bytes 9546853 | solution.py:36
  41.9 1.8 fusion.43
  47.4 1.8 fusion.43
  49.2 1.8 fusion.44
  52.8 1.8 fusion.43
  58.2 1.8 fusion.43
  60.1 1.8 fusion.44
  63.7 1.8 fusion.43
  69.1 1.8 fusion.43
  70.9 1.8 fusion.44
  74.5 1.8 fusion.43
  80.0 1.8 fusion.43
  81.8 1.8 fusion.44
  85.4 1.8 fusion.43
  90.8 1.8 fusion.43
  92.6 1.8 fusion.44
  96.3 1.8 fusion.43
  101.7 1.8 fusion.43
  103.5 1.8 fusion.44
  107.1 1.8 fusion.43
  112.5 1.8 fusion.43
  114.4 1.8 fusion.44
  118.0 1.8 fusion.43
  123.4 1.8 fusion.43
  125.2 1.8 fusion.44
  128.9 1.8 fusion.43
  134.3 1.8 fusion.43
  136.1 1.8 fusion.44
  139.7 1.8 fusion.43
  145.1 1.8 fusion.43
  147.0 1.8 fusion.44
  150.6 1.8 fusion.43
  156.0 1.8 fusion.43
  157.8 1.8 fusion.44
  161.4 1.8 fusion.43
  166.9 1.8 fusion.43
  173.6 3.6 %all-to-all-start.1 = ((bf16[2,1,384,896]{3,2,1,0:T(8,128)(2,1)}), bf16[2,1,384,896]{3,2,1,0:T(8,128)(2,1)S(1)}, u32[]{:S(2)}, u32[]{:S(2)}) async-start(bf16[2,1,384,896]{3,2,1,0:T(8,128)(2,1)} %pad_maximum_fusion), calls=%async_computation.1 | async-start | bytes 2752512 | tf_op jit(solution)/shard_map/all_to_all | solution.py:41
  178.0 16.0 %all-to-all-done.1 = bf16[2,1,384,896]{3,2,1,0:T(8,128)(2,1)S(1)} async-done(((bf16[2,1,384,896]{3,2,1,0:T(8,128)(2,1)}), bf16[2,1,384,896]{3,2,1,0:T(8,128)(2,1)S(1)}, u32[]{:S(2)}, u32[]{:S(2)}) %all-to-all-start.1) | async-done | bytes 1376288 | tf_op jit(solution)/shard_map/all_to_all | solution.py:41
  194.0 2.8 convolution_bitcast_fusion.2
  196.8 27.0 %psum.22 = f32[24,256]{1,0:T(8,128)S(1)} all-reduce(f32[24,256]{1,0:T(8,128)S(1)} %get-tuple-element.39), channel_id=1, replica_groups=mesh['dom'=2,'row'=4,'sub'=2,'rep'=2] {'row','rep'}, use_global_device_ids=true, to_apply=%region_7.8 | all-reduce | flops 6144 | bytes 49152 | tf_op jit(solution)/shard_map/psum | solution.py:46
  223.9 14.8 %all-reduce.3.cloned.1.call-done = f32[24,256,16]{1,2,0:T(8,128)} async-done(((f32[24,256,16]{1,2,0:T(8,128)}), f32[24,256,16]{1,2,0:T(8,128)}) %all-reduce.3.cloned.1.call-update) | async-done | bytes 393232 | tf_op jit(solution)/shard_map/psum | solution.py:46
  238.7 1.8 add_divide_fusion
  242.1 98.6 %all-reduce.5.cloned.1.call-done = f32[768,768]{0,1:T(8,128)} async-done(((f32[768,768]{0,1:T(8,128)}), f32[768,768]{0,1:T(8,128)}) %all-reduce.5.cloned.1.call-update) | async-done | bytes 2359312 | tf_op jit(solution)/shard_map/psum | solution.py:50
  (150 shorter events, 75.4 us)
Async XLA Ops:
  7.2 1.3 copy-start
  12.3 22.2 %all-to-all-start = ((bf16[2,384,896]{2,1,0:T(8,128)(2,1)}), bf16[2,384,896]{2,1,0:T(8,128)(2,1)S(1)}, u32[]{:S(2)}, u32[]{:S(2)}) async-start(bf16[2,384,896]{2,1,0:T(8,128)(2,1)} %bitcast.64), calls=%async_computation | async-start | bytes 2752512 | tf_op jit(solution)/shard_map/all_to_all | solution.py:33
  37.0 3.5 %copy-start.1 = (f32[24,256,16]{1,2,0:T(8,128)S(1)}, f32[24,256,16]{1,2,0:T(8,128)}, u32[]{:S(2)}) copy-start(f32[24,256,16]{1,2,0:T(8,128)} %param.7) | copy-start | bytes 1179652
  173.6 20.5 %all-to-all-start.1 = ((bf16[2,1,384,896]{3,2,1,0:T(8,128)(2,1)}), bf16[2,1,384,896]{3,2,1,0:T(8,128)(2,1)S(1)}, u32[]{:S(2)}, u32[]{:S(2)}) async-start(bf16[2,1,384,896]{3,2,1,0:T(8,128)(2,1)} %pad_maximum_fusion), calls=%async_computation.1 | async-start | bytes 2752512 | tf_op jit(solution)/shard_map/all_to_all | solution.py:41
  177.2 61.5 %all-reduce.3.cloned.1.call-start = ((), (), s32[]{:S(2)}) async-start(), calls=%async_computation.2 | async-start | bytes 786432 | tf_op jit(solution)/shard_map/psum | solution.py:46
  178.0 162.7 %all-reduce.5.cloned.1.call-start = ((), (), s32[]{:S(2)}) async-start(), calls=%async_computation.3 | async-start | bytes 4718592 | tf_op jit(solution)/shard_map/psum | solution.py:50
Sparse Core Ops, SparseCore 0:
  181.0 57.7 all-reduce.2
  242.7 97.9 all-reduce.4
